TPU v7x, 256 devices: a whole 4x4x8 slice. The times are simulated.
256 devices in a mesh: pipe: 8 (over y, x_lo), ctx: 32 (over z, x_hi, core).
Axes of the slice: x: 4 (x_hi: 2, x_lo: 2; x = x_hi * 2 + x_lo), y: 4, z: 8, core: 2. Of those that a mesh axis runs over, the one named last changes fastest.
Arguments:
- queries: bfloat16 [8, 8192, 2048], P('pipe', 'ctx'), may hold values from -70 to 70
- key_rows: bfloat16 [8, 8192, 512], P('pipe', 'ctx'), may hold values from -6 to 6
- value_rows: bfloat16 [8, 8192, 512], P('pipe', 'ctx'), may hold values from -6 to 6
- out_grad: bfloat16 [8, 8192, 2048], P('pipe', 'ctx'), may hold values from -6 to 6
- doc_blocks: int32 [8, 64], P('pipe'), may hold values from 0 to 15, never falling along the last dimension, each value on 1 to 8 neighbouring positions
Outputs:
- attn_out: bfloat16 [8, 8192, 2048], P('pipe', 'ctx')
- grad_query: bfloat16 [8, 8192, 2048], P('pipe', 'ctx')
- grad_key: bfloat16 [8, 8192, 512], P('pipe', 'ctx')
- grad_value: bfloat16 [8, 8192, 512], P('pipe', 'ctx')
Inputs may be any that keep to these rules, and one draw needn't show every extreme that they name: `doc_blocks`: each document is a run of 1 to 8 consecutive blocks; ids never fall along a section's sequence, and in each section some document has exactly 8 blocks.
All inputs are finite; a program needn't handle non-finite values.
Results may differ from a plain program's by a relative error of at most 0.014.
Values may be sent and summed in bfloat16 or wider, within the bound.
A program may use at most 64 MiB of HBM per device.

v0:
```python
import functools
import math

import jax
import jax.numpy as jnp
from jax import lax
from jax.sharding import PartitionSpec as P

HD = 128
H = 16
KVH = 4
BLK = 128
MOST_BLK = 8


def from_behind(value, axis, by):
    peers = lax.axis_size(axis)
    pairs = [(i, i + by) for i in range(peers) if 0 <= i + by < peers]
    return lax.ppermute(value, axis, pairs)


def lookup_doc(positions, doc_row):
    blocks = jnp.arange(doc_row.shape[0], dtype=jnp.int32)
    matches = (positions // BLK)[:, None] == blocks[None, :]
    located = jnp.sum(jnp.where(matches, doc_row[None, :], 0), axis=1)
    return jnp.where(positions >= 0, located, -1)


def attend_group(inputs, visible, score_scale):
    query_group, key_group, value_group, grad_group = inputs
    scores = (
        jnp.einsum("tcd,kd->ctk", query_group, key_group, preferred_element_type=jnp.float32)
        * score_scale
    )
    masked = jnp.where(visible[None], scores, -1e30)
    maxima = jnp.max(masked, axis=-1)
    totals = jnp.sum(jnp.where(visible[None], jnp.exp(masked - maxima[..., None]), 0.0), axis=-1)
    log_norm = maxima + jnp.log(totals)
    probs = jnp.where(visible[None], jnp.exp(scores - log_norm[..., None]), 0.0)
    probs_low = probs.astype(jnp.bfloat16)
    output = jnp.einsum("ctk,kd->tcd", probs_low, value_group, preferred_element_type=jnp.float32)
    out_low = output.astype(jnp.bfloat16)
    row_dots = jnp.einsum(
        "tcd,tcd->ct", grad_group.astype(jnp.float32), out_low.astype(jnp.float32)
    )
    prob_grad = jnp.einsum(
        "tcd,kd->ctk", grad_group, value_group, preferred_element_type=jnp.float32
    )
    score_grad = (probs * (prob_grad - row_dots[..., None])).astype(jnp.bfloat16)
    query_grad = (
        jnp.einsum("ctk,kd->tcd", score_grad, key_group, preferred_element_type=jnp.float32)
        * score_scale
    )
    key_grad = (
        jnp.einsum("ctk,tcd->kd", score_grad, query_group, preferred_element_type=jnp.float32)
        * score_scale
    )
    value_grad = jnp.einsum(
        "ctk,tcd->kd", probs_low, grad_group, preferred_element_type=jnp.float32
    )
    return (out_low, query_grad.astype(jnp.bfloat16), key_grad, value_grad)


def shards(queries, key_rows, value_rows, out_grad, doc_blocks):
    tokens = queries.shape[1]
    group_size = H // KVH
    blocks_dev = tokens // BLK
    reach_shards = (MOST_BLK - 1 + blocks_dev - 1) // blocks_dev
    key_count = (reach_shards + 1) * tokens
    own_keys = key_rows[0]
    own_values = value_rows[0]
    earlier = []
    for hops in range(1, reach_shards + 1):
        earlier.append(from_behind((own_keys, own_values), "ctx", hops))
    ordered = earlier[::-1] + [(own_keys, own_values)]
    key_span = jnp.concatenate([shard_pair[0] for shard_pair in ordered], 0)
    value_span = jnp.concatenate([shard_pair[1] for shard_pair in ordered], 0)
    shard_index = lax.axis_index("ctx")
    key_pos = (shard_index - reach_shards) * tokens + jnp.arange(key_count, dtype=jnp.int32)
    query_pos = shard_index * tokens + jnp.arange(tokens, dtype=jnp.int32)
    doc_row = doc_blocks[0]
    key_doc = lookup_doc(key_pos, doc_row)
    query_doc = lookup_doc(query_pos, doc_row)
    visible = (query_doc[:, None] == key_doc[None, :]) & (key_pos[None, :] <= query_pos[:, None])
    query_groups = queries[0].reshape(tokens, KVH, group_size, HD).transpose(1, 0, 2, 3)
    grad_groups = out_grad[0].reshape(tokens, KVH, group_size, HD).transpose(1, 0, 2, 3)
    key_groups = key_span.reshape(key_count, KVH, HD).transpose(1, 0, 2)
    value_groups = value_span.reshape(key_count, KVH, HD).transpose(1, 0, 2)
    worker = functools.partial(attend_group, visible=visible, score_scale=1.0 / math.sqrt(HD))
    out_low, query_grad, key_grad, value_grad = lax.map(
        worker, (query_groups, key_groups, value_groups, grad_groups)
    )
    attn_out = out_low.transpose(1, 0, 2, 3).reshape(1, tokens, H * HD)
    query_final = query_grad.transpose(1, 0, 2, 3).reshape(1, tokens, H * HD)
    key_terms = key_grad.transpose(1, 0, 2).reshape(key_count, KVH * HD)
    value_terms = value_grad.transpose(1, 0, 2).reshape(key_count, KVH * HD)
    key_parts = [
        key_terms[index * tokens : (index + 1) * tokens] for index in range(reach_shards + 1)
    ]
    value_parts = [
        value_terms[index * tokens : (index + 1) * tokens] for index in range(reach_shards + 1)
    ]
    summed_keys = key_parts[reach_shards]
    summed_values = value_parts[reach_shards]
    for hops in range(1, reach_shards + 1):
        back_keys, back_values = from_behind(
            (
                key_parts[reach_shards - hops].astype(jnp.bfloat16),
                value_parts[reach_shards - hops].astype(jnp.bfloat16),
            ),
            "ctx",
            -hops,
        )
        summed_keys = summed_keys + back_keys.astype(jnp.float32)
        summed_values = summed_values + back_values.astype(jnp.float32)
    key_final = summed_keys.astype(jnp.bfloat16).reshape(1, tokens, KVH * HD)
    value_final = summed_values.astype(jnp.bfloat16).reshape(1, tokens, KVH * HD)
    sent_query, sent_keys, sent_values = from_behind(
        (query_final, key_final, value_final), "pipe", -1
    )
    return (attn_out, sent_query, sent_keys, sent_values)


def solution(mesh):
    placed = (
        P("pipe", "ctx", None),
        P("pipe", "ctx", None),
        P("pipe", "ctx", None),
        P("pipe", "ctx", None),
        P("pipe", None),
    )
    return jax.shard_map(
        shards,
        mesh=mesh,
        in_specs=placed,
        out_specs=(
            P("pipe", "ctx", None),
            P("pipe", "ctx", None),
            P("pipe", "ctx", None),
            P("pipe", "ctx", None),
        ),
        check_vma=False,
    )
```

profile of v0, /device:TPU:185, one launch (start us, length us, event | category | flops | bytes accessed | tf_op | source)
XLA Modules:
  0.0 190.3 jit_solution(9065456627193317071)
XLA Ops:
  1.8 2.6 %collective-permute-start.4 = (bf16[256,512]{0,1:T(8,128)(2,1)S(1)}, bf16[256,512]{0,1:T(8,128)(2,1)S(1)}, u32[]{:S(2)}, u32[]{:S(2)}) collective-permute-start(bf16[256,512]{0,1:T(8,128)(2,1)S(1)} %bitcast.256), channel_id=1, source_target_pairs={{0,4},{1,5},{2,6},{3,7},{4,8},{5,9},{6,10},{7,11},{8,12},{9,13},{1... | collective-permute-start | bytes 786440 | tf_op jit(solution)/shard_map/ppermute | solution.py:19
  4.5 3.5 %collective-permute-start.5 = (bf16[256,512]{0,1:T(8,128)(2,1)S(1)}, bf16[256,512]{0,1:T(8,128)(2,1)}, u32[]{:S(2)}, u32[]{:S(2)}) collective-permute-start(bf16[256,512]{0,1:T(8,128)(2,1)S(1)} %bitcast.257), channel_id=1, source_target_pairs={{0,3},{1,4},{2,5},{3,6},{4,7},{5,8},{6,9},{7,10},{8,11},{9,12},{10... | collective-permute-start | bytes 786440 | tf_op jit(solution)/shard_map/ppermute | solution.py:19
  8.0 4.7 %collective-permute-start.6 = (bf16[256,512]{0,1:T(8,128)(2,1)S(1)}, bf16[256,512]{0,1:T(8,128)(2,1)}, u32[]{:S(2)}, u32[]{:S(2)}) collective-permute-start(bf16[256,512]{0,1:T(8,128)(2,1)S(1)} %bitcast.258), channel_id=1, source_target_pairs={{0,2},{1,3},{2,4},{3,5},{4,6},{5,7},{6,8},{7,9},{8,10},{9,11},{10,... | collective-permute-start | bytes 786440 | tf_op jit(solution)/shard_map/ppermute | solution.py:19
  12.7 4.3 %collective-permute-start.7 = (bf16[256,512]{0,1:T(8,128)(2,1)S(1)}, bf16[256,512]{0,1:T(8,128)(2,1)}, u32[]{:S(2)}, u32[]{:S(2)}) collective-permute-start(bf16[256,512]{0,1:T(8,128)(2,1)S(1)} %bitcast.259), channel_id=1, source_target_pairs={{0,1},{1,2},{2,3},{3,4},{4,5},{5,6},{6,7},{7,8},{8,9},{9,10},{10,1... | collective-permute-start | bytes 786440 | tf_op jit(solution)/shard_map/ppermute | solution.py:19
  26.4 11.4 %collective-permute-start.2 = (bf16[256,512]{1,0:T(8,128)(2,1)S(1)}, bf16[256,512]{1,0:T(8,128)(2,1)}, u32[]{:S(2)}, u32[]{:S(2)}) collective-permute-start(bf16[256,512]{1,0:T(8,128)(2,1)S(1)} %bitcast.268), channel_id=1, source_target_pairs={{0,2},{1,3},{2,4},{3,5},{4,6},{5,7},{6,8},{7,9},{8,10},{9,11},{10,... | collective-permute-start | bytes 786440 | tf_op jit(solution)/shard_map/ppermute | solution.py:19
  50.9 64.6 %while.17 = (s32[]{:T(128)}, bf16[4,256,4,128]{1,3,2,0:T(8,128)(2,1)}, bf16[4,256,4,128]{1,3,2,0:T(8,128)(2,1)}, f32[4,1280,128]{2,1,0:T(8,128)}, f32[4,1280,128...) while((s32[]{:T(128)}, ...), condition=%wide.region_5.6_spmd.clone, body=%wide.region_2.5_spmd.clone.sunk | while | flops 2038921216 | bytes 79886584 | solution.py:90
  56.6 2.8 %bitcast_dynamic-update-slice_fusion.2 = (bf16[4,256,4,128]{1,3,2,0:T(8,128)(2,1)}, bf16[128,4,256]{2,0,1:T(8,128)(2,1)S(1)}) fusion(bf16[4,256,4,128]{1,3,2,0:T(8,128)(2,1)} %get-tuple-element.265, s32[]{:T(128)} %get-tuple-element.264, f32[1280,256,4]{1,0,2:T(8,128)S(1)} %get-tuple-element.246, f32[4,256]{1,0:T(4,128)S(1)} %log_add_fusion.2, ...), kind=kOutput, calls=%fused_computation.37.clone.1 | convolution fusion | flops 339607552 | bytes 6427648 | tf_op jit(solution)/shard_map/while/body/eval_jaxpr/ctk,kd->tcd/dot_general | solution.py:41
  59.9 4.2 %fusion.77 = bf16[4,256,1280]{1,2,0:T(8,128)(2,1)S(1)} fusion(f32[1280,256,4]{1,0,2:T(8,128)} %copy-done, f32[4,256]{1,0:T(4,128)S(1)} %multiply_reduce_fusion.2, f32[4,256]{1,0:T(4,128)S(1)} %log_add_fusion.2, pred[256,1280]{0,1:T(8,128)(4,1)S(1)} %compare_and_fusion.2, bf16[4,1280,128]{1,2,0:T(8,128)(2,1)} %get-tuple-element.283, ...), kind=kOutput, calls=%fused_computation.3.clone.1 | convolution fusion | flops 342097920 | bytes 8791040 | tf_op jit(solution)/shard_map/while/body/eval_jaxpr/tcd,kd->ctk/dot_general | solution.py:46
  72.8 2.8 %bitcast_dynamic-update-slice_fusion.2 = (bf16[4,256,4,128]{1,3,2,0:T(8,128)(2,1)}, bf16[128,4,256]{2,0,1:T(8,128)(2,1)S(1)}) fusion(bf16[4,256,4,128]{1,3,2,0:T(8,128)(2,1)} %get-tuple-element.265, s32[]{:T(128)} %get-tuple-element.264, f32[1280,256,4]{1,0,2:T(8,128)S(1)} %get-tuple-element.246, f32[4,256]{1,0:T(4,128)S(1)} %log_add_fusion.2, ...), kind=kOutput, calls=%fused_computation.37.clone.1 | convolution fusion | flops 339607552 | bytes 6427648 | tf_op jit(solution)/shard_map/while/body/eval_jaxpr/ctk,kd->tcd/dot_general | solution.py:41
  76.1 4.2 %fusion.77 = bf16[4,256,1280]{1,2,0:T(8,128)(2,1)S(1)} fusion(f32[1280,256,4]{1,0,2:T(8,128)} %copy-done, f32[4,256]{1,0:T(4,128)S(1)} %multiply_reduce_fusion.2, f32[4,256]{1,0:T(4,128)S(1)} %log_add_fusion.2, pred[256,1280]{0,1:T(8,128)(4,1)S(1)} %compare_and_fusion.2, bf16[4,1280,128]{1,2,0:T(8,128)(2,1)} %get-tuple-element.283, ...), kind=kOutput, calls=%fused_computation.3.clone.1 | convolution fusion | flops 342097920 | bytes 8791040 | tf_op jit(solution)/shard_map/while/body/eval_jaxpr/tcd,kd->ctk/dot_general | solution.py:46
  88.9 2.8 %bitcast_dynamic-update-slice_fusion.2 = (bf16[4,256,4,128]{1,3,2,0:T(8,128)(2,1)}, bf16[128,4,256]{2,0,1:T(8,128)(2,1)S(1)}) fusion(bf16[4,256,4,128]{1,3,2,0:T(8,128)(2,1)} %get-tuple-element.265, s32[]{:T(128)} %get-tuple-element.264, f32[1280,256,4]{1,0,2:T(8,128)S(1)} %get-tuple-element.246, f32[4,256]{1,0:T(4,128)S(1)} %log_add_fusion.2, ...), kind=kOutput, calls=%fused_computation.37.clone.1 | convolution fusion | flops 339607552 | bytes 6427648 | tf_op jit(solution)/shard_map/while/body/eval_jaxpr/ctk,kd->tcd/dot_general | solution.py:41
  92.2 4.2 %fusion.77 = bf16[4,256,1280]{1,2,0:T(8,128)(2,1)S(1)} fusion(f32[1280,256,4]{1,0,2:T(8,128)} %copy-done, f32[4,256]{1,0:T(4,128)S(1)} %multiply_reduce_fusion.2, f32[4,256]{1,0:T(4,128)S(1)} %log_add_fusion.2, pred[256,1280]{0,1:T(8,128)(4,1)S(1)} %compare_and_fusion.2, bf16[4,1280,128]{1,2,0:T(8,128)(2,1)} %get-tuple-element.283, ...), kind=kOutput, calls=%fused_computation.3.clone.1 | convolution fusion | flops 342097920 | bytes 8791040 | tf_op jit(solution)/shard_map/while/body/eval_jaxpr/tcd,kd->ctk/dot_general | solution.py:46
  105.0 2.8 %bitcast_dynamic-update-slice_fusion.2 = (bf16[4,256,4,128]{1,3,2,0:T(8,128)(2,1)}, bf16[128,4,256]{2,0,1:T(8,128)(2,1)S(1)}) fusion(bf16[4,256,4,128]{1,3,2,0:T(8,128)(2,1)} %get-tuple-element.265, s32[]{:T(128)} %get-tuple-element.264, f32[1280,256,4]{1,0,2:T(8,128)S(1)} %get-tuple-element.246, f32[4,256]{1,0:T(4,128)S(1)} %log_add_fusion.2, ...), kind=kOutput, calls=%fused_computation.37.clone.1 | convolution fusion | flops 339607552 | bytes 6427648 | tf_op jit(solution)/shard_map/while/body/eval_jaxpr/ctk,kd->tcd/dot_general | solution.py:41
  108.3 4.2 %fusion.77 = bf16[4,256,1280]{1,2,0:T(8,128)(2,1)S(1)} fusion(f32[1280,256,4]{1,0,2:T(8,128)} %copy-done, f32[4,256]{1,0:T(4,128)S(1)} %multiply_reduce_fusion.2, f32[4,256]{1,0:T(4,128)S(1)} %log_add_fusion.2, pred[256,1280]{0,1:T(8,128)(4,1)S(1)} %compare_and_fusion.2, bf16[4,1280,128]{1,2,0:T(8,128)(2,1)} %get-tuple-element.283, ...), kind=kOutput, calls=%fused_computation.3.clone.1 | convolution fusion | flops 342097920 | bytes 8791040 | tf_op jit(solution)/shard_map/while/body/eval_jaxpr/tcd,kd->ctk/dot_general | solution.py:46
  118.2 2.6 %collective-permute-start.14 = (bf16[256,512]{1,0:T(8,128)(2,1)}, bf16[256,512]{1,0:T(8,128)(2,1)}, u32[]{:S(2)}, u32[]{:S(2)}) collective-permute-start(bf16[256,512]{1,0:T(8,128)(2,1)} %bitcast.198), channel_id=1, source_target_pairs={{1,0},{2,1},{3,2},{4,3},{5,4},{6,5},{7,6},{8,7},{9,8},{10,9},{11,1... | collective-permute-start | bytes 786440 | tf_op jit(solution)/shard_map/ppermute | solution.py:19
  121.5 3.8 %collective-permute-start.15 = (bf16[256,512]{1,0:T(8,128)(2,1)}, bf16[256,512]{1,0:T(8,128)(2,1)}, u32[]{:S(2)}, u32[]{:S(2)}) collective-permute-start(bf16[256,512]{1,0:T(8,128)(2,1)} %bitcast.197), channel_id=1, source_target_pairs={{2,0},{3,1},{4,2},{5,3},{6,4},{7,5},{8,6},{9,7},{10,8},{11,9},{12,... | collective-permute-start | bytes 786440 | tf_op jit(solution)/shard_map/ppermute | solution.py:19
  126.0 7.4 %collective-permute-start.16 = (bf16[256,512]{1,0:T(8,128)(2,1)}, bf16[256,512]{1,0:T(8,128)(2,1)}, u32[]{:S(2)}, u32[]{:S(2)}) collective-permute-start(bf16[256,512]{1,0:T(8,128)(2,1)} %bitcast.196), channel_id=1, source_target_pairs={{3,0},{4,1},{5,2},{6,3},{7,4},{8,5},{9,6},{10,7},{11,8},{12,9},{13... | collective-permute-start | bytes 786440 | tf_op jit(solution)/shard_map/ppermute | solution.py:19
  137.0 2.4 %collective-permute-start.8 = (bf16[1,256,2048]{2,1,0:T(8,128)(2,1)S(1)}, bf16[1,256,2048]{2,1,0:T(8,128)(2,1)S(1)}, u32[]{:S(2)}, u32[]{:S(2)}) collective-permute-start(bf16[1,256,2048]{2,1,0:T(8,128)(2,1)S(1)} %copy.97), channel_id=1, source_target_pairs={{32,0},{64,32},{96,64},{128,96},{160,128},{192,160},{224,192},{33,... | collective-permute-start | bytes 3145736 | tf_op jit(solution)/shard_map/ppermute | solution.py:19
  139.7 2.4 %collective-permute-start.10 = (bf16[256,512]{1,0:T(8,128)(2,1)S(1)}, bf16[256,512]{1,0:T(8,128)(2,1)S(1)}, u32[]{:S(2)}, u32[]{:S(2)}) collective-permute-start(bf16[256,512]{1,0:T(8,128)(2,1)S(1)} %bitcast.274), channel_id=1, source_target_pairs={{2,0},{3,1},{4,2},{5,3},{6,4},{7,5},{8,6},{9,7},{10,8},{11,9},{12,... | collective-permute-start | bytes 786440 | tf_op jit(solution)/shard_map/ppermute | solution.py:19
  142.1 2.5 %collective-permute-start.11 = (bf16[256,512]{1,0:T(8,128)(2,1)S(1)}, bf16[256,512]{1,0:T(8,128)(2,1)S(1)}, u32[]{:S(2)}, u32[]{:S(2)}) collective-permute-start(bf16[256,512]{1,0:T(8,128)(2,1)S(1)} %bitcast.273), channel_id=1, source_target_pairs={{3,0},{4,1},{5,2},{6,3},{7,4},{8,5},{9,6},{10,7},{11,8},{12,9},{13... | collective-permute-start | bytes 786440 | tf_op jit(solution)/shard_map/ppermute | solution.py:19
  146.6 2.3 %collective-permute-start.9 = (bf16[256,512]{1,0:T(8,128)(2,1)S(1)}, bf16[256,512]{1,0:T(8,128)(2,1)S(1)}, u32[]{:S(2)}, u32[]{:S(2)}) collective-permute-start(bf16[256,512]{1,0:T(8,128)(2,1)S(1)} %bitcast.271), channel_id=1, source_target_pairs={{1,0},{2,1},{3,2},{4,3},{5,4},{6,5},{7,6},{8,7},{9,8},{10,9},{11,1... | collective-permute-start | bytes 786440 | tf_op jit(solution)/shard_map/ppermute | solution.py:19
  151.1 17.4 %collective-permute-done.10 = bf16[256,512]{1,0:T(8,128)(2,1)S(1)} collective-permute-done((bf16[256,512]{1,0:T(8,128)(2,1)S(1)}, bf16[256,512]{1,0:T(8,128)(2,1)S(1)}, u32[]{:S(2)}, u32[]{:S(2)}) %collective-permute-start.10) | collective-permute-done | bytes 262176 | tf_op jit(solution)/shard_map/ppermute | solution.py:19
  170.4 5.4 %collective-permute-done.9 = bf16[256,512]{1,0:T(8,128)(2,1)S(1)} collective-permute-done((bf16[256,512]{1,0:T(8,128)(2,1)S(1)}, bf16[256,512]{1,0:T(8,128)(2,1)S(1)}, u32[]{:S(2)}, u32[]{:S(2)}) %collective-permute-start.9) | collective-permute-done | bytes 262176 | tf_op jit(solution)/shard_map/ppermute | solution.py:19
  181.0 5.9 %collective-permute-done.13 = bf16[1,256,512]{2,1,0:T(8,128)(2,1)S(1)} collective-permute-done((bf16[1,256,512]{2,1,0:T(8,128)(2,1)}, bf16[1,256,512]{2,1,0:T(8,128)(2,1)S(1)}, u32[]{:S(2)}, u32[]{:S(2)}) %collective-permute-start.13) | collective-permute-done | bytes 262176 | tf_op jit(solution)/shard_map/ppermute | solution.py:19
  (160 shorter events, 82.6 us)
Async XLA Ops:
  0.6 23.8 %copy-start.8 = (bf16[1,256,512]{2,1,0:T(8,128)(2,1)S(1)}, bf16[1,256,512]{2,1,0:T(8,128)(2,1)}, u32[]{:S(2)}) copy-start(bf16[1,256,512]{2,1,0:T(8,128)(2,1)} %param.9) | copy-start | bytes 786436
  0.6 22.5 %copy-start.5 = (bf16[1,256,2048]{2,1,0:T(8,128)(2,1)S(1)}, bf16[1,256,2048]{2,1,0:T(8,128)(2,1)}, u32[]{:S(2)}) copy-start(bf16[1,256,2048]{2,1,0:T(8,128)(2,1)} %param.10) | copy-start | bytes 3145732
  1.8 22.6 %collective-permute-start.4 = (bf16[256,512]{0,1:T(8,128)(2,1)S(1)}, bf16[256,512]{0,1:T(8,128)(2,1)S(1)}, u32[]{:S(2)}, u32[]{:S(2)}) collective-permute-start(bf16[256,512]{0,1:T(8,128)(2,1)S(1)} %bitcast.256), channel_id=1, source_target_pairs={{0,4},{1,5},{2,6},{3,7},{4,8},{5,9},{6,10},{7,11},{8,12},{9,13},{1... | collective-permute-start | bytes 786440 | tf_op jit(solution)/shard_map/ppermute | solution.py:19
  4.5 35.2 %collective-permute-start.5 = (bf16[256,512]{0,1:T(8,128)(2,1)S(1)}, bf16[256,512]{0,1:T(8,128)(2,1)}, u32[]{:S(2)}, u32[]{:S(2)}) collective-permute-start(bf16[256,512]{0,1:T(8,128)(2,1)S(1)} %bitcast.257), channel_id=1, source_target_pairs={{0,3},{1,4},{2,5},{3,6},{4,7},{5,8},{6,9},{7,10},{8,11},{9,12},{10... | collective-permute-start | bytes 786440 | tf_op jit(solution)/shard_map/ppermute | solution.py:19
  8.0 34.6 %collective-permute-start.6 = (bf16[256,512]{0,1:T(8,128)(2,1)S(1)}, bf16[256,512]{0,1:T(8,128)(2,1)}, u32[]{:S(2)}, u32[]{:S(2)}) collective-permute-start(bf16[256,512]{0,1:T(8,128)(2,1)S(1)} %bitcast.258), channel_id=1, source_target_pairs={{0,2},{1,3},{2,4},{3,5},{4,6},{5,7},{6,8},{7,9},{8,10},{9,11},{10,... | collective-permute-start | bytes 786440 | tf_op jit(solution)/shard_map/ppermute | solution.py:19
  12.7 30.9 %collective-permute-start.7 = (bf16[256,512]{0,1:T(8,128)(2,1)S(1)}, bf16[256,512]{0,1:T(8,128)(2,1)}, u32[]{:S(2)}, u32[]{:S(2)}) collective-permute-start(bf16[256,512]{0,1:T(8,128)(2,1)S(1)} %bitcast.259), channel_id=1, source_target_pairs={{0,1},{1,2},{2,3},{3,4},{4,5},{5,6},{6,7},{7,8},{8,9},{9,10},{10,1... | collective-permute-start | bytes 786440 | tf_op jit(solution)/shard_map/ppermute | solution.py:19
  17.0 9.4 %collective-permute-start = (bf16[256,512]{1,0:T(8,128)(2,1)}, bf16[256,512]{1,0:T(8,128)(2,1)}, u32[]{:S(2)}, u32[]{:S(2)}) collective-permute-start(bf16[256,512]{1,0:T(8,128)(2,1)} %bitcast.266), channel_id=1, source_target_pairs={{0,4},{1,5},{2,6},{3,7},{4,8},{5,9},{6,10},{7,11},{8,12},{9,13},{1... | collective-permute-start | bytes 786440 | tf_op jit(solution)/shard_map/ppermute | solution.py:19
  24.5 20.1 %collective-permute-start.1 = (bf16[256,512]{1,0:T(8,128)(2,1)S(1)}, bf16[256,512]{1,0:T(8,128)(2,1)}, u32[]{:S(2)}, u32[]{:S(2)}) collective-permute-start(bf16[256,512]{1,0:T(8,128)(2,1)S(1)} %bitcast.267), channel_id=1, source_target_pairs={{0,3},{1,4},{2,5},{3,6},{4,7},{5,8},{6,9},{7,10},{8,11},{9,12},{10... | collective-permute-start | bytes 786440 | tf_op jit(solution)/shard_map/ppermute | solution.py:19
  26.4 19.3 %collective-permute-start.2 = (bf16[256,512]{1,0:T(8,128)(2,1)S(1)}, bf16[256,512]{1,0:T(8,128)(2,1)}, u32[]{:S(2)}, u32[]{:S(2)}) collective-permute-start(bf16[256,512]{1,0:T(8,128)(2,1)S(1)} %bitcast.268), channel_id=1, source_target_pairs={{0,2},{1,3},{2,4},{3,5},{4,6},{5,7},{6,8},{7,9},{8,10},{9,11},{10,... | collective-permute-start | bytes 786440 | tf_op jit(solution)/shard_map/ppermute | solution.py:19
  39.7 8.6 %collective-permute-start.3 = (bf16[256,512]{1,0:T(8,128)(2,1)S(1)}, bf16[256,512]{1,0:T(8,128)(2,1)}, u32[]{:S(2)}, u32[]{:S(2)}) collective-permute-start(bf16[256,512]{1,0:T(8,128)(2,1)S(1)} %bitcast.269), channel_id=1, source_target_pairs={{0,1},{1,2},{2,3},{3,4},{4,5},{5,6},{6,7},{7,8},{8,9},{9,10},{10,1... | collective-permute-start | bytes 786440 | tf_op jit(solution)/shard_map/ppermute | solution.py:19
  117.3 18.8 %copy-start.4 = (f32[4,1280,128]{2,1,0:T(8,128)S(1)}, f32[4,1280,128]{2,1,0:T(8,128)}, u32[]{:S(2)}) copy-start(f32[4,1280,128]{2,1,0:T(8,128)} %get-tuple-element.61) | copy-start | bytes 7864324
  118.2 21.5 %collective-permute-start.14 = (bf16[256,512]{1,0:T(8,128)(2,1)}, bf16[256,512]{1,0:T(8,128)(2,1)}, u32[]{:S(2)}, u32[]{:S(2)}) collective-permute-start(bf16[256,512]{1,0:T(8,128)(2,1)} %bitcast.198), channel_id=1, source_target_pairs={{1,0},{2,1},{3,2},{4,3},{5,4},{6,5},{7,6},{8,7},{9,8},{10,9},{11,1... | collective-permute-start | bytes 786440 | tf_op jit(solution)/shard_map/ppermute | solution.py:19
  121.5 14.8 %copy-start.7 = (bf16[4,256,4,128]{1,3,2,0:T(8,128)(2,1)S(1)}, bf16[4,256,4,128]{1,3,2,0:T(8,128)(2,1)}, u32[]{:S(2)}) copy-start(bf16[4,256,4,128]{1,3,2,0:T(8,128)(2,1)} %get-tuple-element.60) | copy-start | bytes 3145732
  121.5 20.6 %collective-permute-start.15 = (bf16[256,512]{1,0:T(8,128)(2,1)}, bf16[256,512]{1,0:T(8,128)(2,1)}, u32[]{:S(2)}, u32[]{:S(2)}) collective-permute-start(bf16[256,512]{1,0:T(8,128)(2,1)} %bitcast.197), channel_id=1, source_target_pairs={{2,0},{3,1},{4,2},{5,3},{6,4},{7,5},{8,6},{9,7},{10,8},{11,9},{12,... | collective-permute-start | bytes 786440 | tf_op jit(solution)/shard_map/ppermute | solution.py:19
  126.0 18.6 %collective-permute-start.16 = (bf16[256,512]{1,0:T(8,128)(2,1)}, bf16[256,512]{1,0:T(8,128)(2,1)}, u32[]{:S(2)}, u32[]{:S(2)}) collective-permute-start(bf16[256,512]{1,0:T(8,128)(2,1)} %bitcast.196), channel_id=1, source_target_pairs={{3,0},{4,1},{5,2},{6,3},{7,4},{8,5},{9,6},{10,7},{11,8},{12,9},{13... | collective-permute-start | bytes 786440 | tf_op jit(solution)/shard_map/ppermute | solution.py:19
  134.2 12.3 %collective-permute-start.17 = (bf16[256,512]{1,0:T(8,128)(2,1)}, bf16[256,512]{1,0:T(8,128)(2,1)}, u32[]{:S(2)}, u32[]{:S(2)}) collective-permute-start(bf16[256,512]{1,0:T(8,128)(2,1)} %bitcast.195), channel_id=1, source_target_pairs={{4,0},{5,1},{6,2},{7,3},{8,4},{9,5},{10,6},{11,7},{12,8},{13,9},{1... | collective-permute-start | bytes 786440 | tf_op jit(solution)/shard_map/ppermute | solution.py:19
  137.0 50.0 %collective-permute-start.8 = (bf16[1,256,2048]{2,1,0:T(8,128)(2,1)S(1)}, bf16[1,256,2048]{2,1,0:T(8,128)(2,1)S(1)}, u32[]{:S(2)}, u32[]{:S(2)}) collective-permute-start(bf16[1,256,2048]{2,1,0:T(8,128)(2,1)S(1)} %copy.97), channel_id=1, source_target_pairs={{32,0},{64,32},{96,64},{128,96},{160,128},{192,160},{224,192},{33,... | collective-permute-start | bytes 3145736 | tf_op jit(solution)/shard_map/ppermute | solution.py:19
  139.6 40.1 %copy-start.6 = (bf16[4,256,4,128]{1,3,2,0:T(8,128)(2,1)S(1)}, bf16[4,256,4,128]{1,3,2,0:T(8,128)(2,1)}, u32[]{:S(2)}) copy-start(bf16[4,256,4,128]{1,3,2,0:T(8,128)(2,1)} %get-tuple-element.59) | copy-start | bytes 3145732
  139.7 28.7 %collective-permute-start.10 = (bf16[256,512]{1,0:T(8,128)(2,1)S(1)}, bf16[256,512]{1,0:T(8,128)(2,1)S(1)}, u32[]{:S(2)}, u32[]{:S(2)}) collective-permute-start(bf16[256,512]{1,0:T(8,128)(2,1)S(1)} %bitcast.274), channel_id=1, source_target_pairs={{2,0},{3,1},{4,2},{5,3},{6,4},{7,5},{8,6},{9,7},{10,8},{11,9},{12,... | collective-permute-start | bytes 786440 | tf_op jit(solution)/shard_map/ppermute | solution.py:19
  142.1 28.3 %collective-permute-start.11 = (bf16[256,512]{1,0:T(8,128)(2,1)S(1)}, bf16[256,512]{1,0:T(8,128)(2,1)S(1)}, u32[]{:S(2)}, u32[]{:S(2)}) collective-permute-start(bf16[256,512]{1,0:T(8,128)(2,1)S(1)} %bitcast.273), channel_id=1, source_target_pairs={{3,0},{4,1},{5,2},{6,3},{7,4},{8,5},{9,6},{10,7},{11,8},{12,9},{13... | collective-permute-start | bytes 786440 | tf_op jit(solution)/shard_map/ppermute | solution.py:19
  144.6 25.8 %collective-permute-start.12 = (bf16[256,512]{1,0:T(8,128)(2,1)S(1)}, bf16[256,512]{1,0:T(8,128)(2,1)S(1)}, u32[]{:S(2)}, u32[]{:S(2)}) collective-permute-start(bf16[256,512]{1,0:T(8,128)(2,1)S(1)} %bitcast.272), channel_id=1, source_target_pairs={{4,0},{5,1},{6,2},{7,3},{8,4},{9,5},{10,6},{11,7},{12,8},{13,9},{1... | collective-permute-start | bytes 786440 | tf_op jit(solution)/shard_map/ppermute | solution.py:19
  146.6 29.2 %collective-permute-start.9 = (bf16[256,512]{1,0:T(8,128)(2,1)S(1)}, bf16[256,512]{1,0:T(8,128)(2,1)S(1)}, u32[]{:S(2)}, u32[]{:S(2)}) collective-permute-start(bf16[256,512]{1,0:T(8,128)(2,1)S(1)} %bitcast.271), channel_id=1, source_target_pairs={{1,0},{2,1},{3,2},{4,3},{5,4},{6,5},{7,6},{8,7},{9,8},{10,9},{11,1... | collective-permute-start | bytes 786440 | tf_op jit(solution)/shard_map/ppermute | solution.py:19
  168.5 12.6 %collective-permute-start.18 = (bf16[1,256,512]{2,1,0:T(8,128)(2,1)}, bf16[1,256,512]{2,1,0:T(8,128)(2,1)}, u32[]{:S(2)}, u32[]{:S(2)}) collective-permute-start(bf16[1,256,512]{2,1,0:T(8,128)(2,1)} %fusion.47), channel_id=1, source_target_pairs={{32,0},{64,32},{96,64},{128,96},{160,128},{192,160},{224,192},{33,... | collective-permute-start | bytes 786440 | tf_op jit(solution)/shard_map/ppermute | solution.py:19
  177.7 9.3 %collective-permute-start.13 = (bf16[1,256,512]{2,1,0:T(8,128)(2,1)}, bf16[1,256,512]{2,1,0:T(8,128)(2,1)S(1)}, u32[]{:S(2)}, u32[]{:S(2)}) collective-permute-start(bf16[1,256,512]{2,1,0:T(8,128)(2,1)} %fusion.46), channel_id=1, source_target_pairs={{32,0},{64,32},{96,64},{128,96},{160,128},{192,160},{224,192},{33,... | collective-permute-start | bytes 786440 | tf_op jit(solution)/shard_map/ppermute | solution.py:19
  (16 other events, 53.0 us)
where the time goes:
time: 192 us; the launch traced here: 190 us
  starting transfers between devices  63.3 us (33%)
  matrix products  50.9 us (27%)
  local copies, waits for them, and re-layouts  29.8 us (16%)
  waiting for transfers between devices  28.7 us (15%)
  other arithmetic  16.2 us (8%)
    ppermute x19, starting transfers between devices, from_behind(): return lax.ppermute(value, axis, pairs)  63.3 us
    ppermute x19, waiting for transfers between devices, from_behind(): return lax.ppermute(value, axis, pairs)  28.7 us
    dot_general x4, matrix products, attend_group(): jnp.einsum('tcd,kd->ctk', grad_group, value_group, preferred_element_type...  16.6 us
    unnamed x27, local copies, waits for them, and re-layouts  14.5 us
    dot_general x4, matrix products, attend_group(): jnp.einsum('ctk,kd->tcd', probs_low, value_group, preferred_element_type=...  11.1 us
    dot_general x4, matrix products, attend_group(): jnp.einsum('ctk,tcd->kd', probs_low, grad_group, preferred_element_type=j...  7.3 us
    dot_general x4, matrix products, attend_group(): jnp.einsum('ctk,tcd->kd', score_grad, query_group, preferred_element_type...  6.83 us
    dot_general x4, matrix products, attend_group(): jnp.einsum('ctk,kd->tcd', score_grad, key_group, preferred_element_type=j...  4.88 us
  transfers between devices with their start and end apart: 19, of which 3 were waited for; matrix products, arithmetic and copies ran while one was open for 12% of the time, Pallas kernels for 0%

commit v1 on v0

v1 whole, which is shorter than its diff:
```python
import functools
import math

import jax
import jax.numpy as jnp
from jax import lax
from jax.experimental import pallas as pl
from jax.experimental.pallas import tpu as pltpu
from jax.sharding import PartitionSpec as P

MESH = pl.DeviceIdType.MESH
BF16 = jnp.bfloat16
F32 = jnp.float32
BLK = 128
SCALE = 1.0 / math.sqrt(128.0)
SCALE2 = SCALE * math.log2(math.e)
HIDE = 1e30
ROWS = 11 * BLK
WIN = 8 * BLK


def dot(a, b, dims):
    return lax.dot_general(a, b, (dims, ((), ())), preferred_element_type=F32)


def kernel(
    sections, shards,
    doc_ref, q_hbm, k_hbm, v_hbm, g_hbm,
    out_ref, gq_ref, gk_ref, gv_ref,
    qb_ref, gb_ref, kv_ref, kvt_ref, s_ref, dp_ref, e_ref, ds_ref, acc_ref, dgn_ref, q2_ref,
    o_st, dq_st, c2_st, c1_st, own_st, c2_rx, nxt_rx, own_rx,
    io_loc, io_snd, io_rcv, kv_loc, kv_snd, kv_rcv, o_sem, o_rcv, dq_snd, dq_rcv,
    c2_snd, c2_rcv, c1_snd, c1_rcv, own_snd, own_rcv,
):
    p = lax.axis_index("pipe")
    dev = lax.axis_index("ctx")
    core = lax.rem(dev, 2)
    chip = lax.div(dev, 2)
    chips = shards // 2
    nxt_p = lax.rem(p + 1, sections)
    prv_p = lax.rem(p + sections - 1, sections)

    def at(section, hop, which):
        return (section, 2 * lax.rem(chip + hop + chips, chips) + which)

    partner = (p, 2 * chip + 1 - core)
    barrier = pltpu.get_barrier_semaphore()
    sources = [partner, at(p, 2, core)]
    for which in range(2):
        sources += [at(p, -1, which), at(p, -2, which), at(nxt_p, 0, which), at(nxt_p, 1, which)]
    for source in sources:
        pl.semaphore_signal(barrier, inc=1, device_id=source, device_id_type=MESH)
    pl.semaphore_wait(barrier, len(sources))

    def remote(src, dst, snd, rcv, target):
        return pltpu.make_async_remote_copy(
            src_ref=src, dst_ref=dst, send_sem=snd, recv_sem=rcv,
            device_id=target, device_id_type=MESH,
        )

    def kv_cols(ref, rows, which, g):
        return ref.at[0, rows, pl.ds(pl.multiple_of((2 * which + g) * BLK, BLK), BLK)]

    kv_hbm = (k_hbm, v_hbm)
    io_hbm = (q_hbm, g_hbm)
    io_buf = (qb_ref, gb_ref)
    mine = pl.ds(pl.multiple_of(core * 256, 256), 256)
    whole = pl.ds(0, 256)

    def io_copies(g):
        copies = []
        for i in range(2):
            src = lambda which: io_hbm[i].at[0, :, pl.ds(pl.multiple_of(which * 1024 + g * 512, 512), 512)]
            dst = io_buf[i].at[g, mine, :]
            copies.append(pltpu.make_async_copy(src(core), dst, io_loc.at[g, i]))
            copies.append(remote(src(1 - core), dst, io_snd.at[g, i], io_rcv.at[g, i], partner))
        return copies

    def kv_own(g):
        copies = []
        for i in range(2):
            dst = kv_ref.at[i, g, pl.ds(pl.multiple_of(896 + core * 256, 128), 256), :]
            copies.append(pltpu.make_async_copy(kv_cols(kv_hbm[i], whole, core, g), dst, kv_loc.at[g, i]))
            copies.append(
                remote(kv_cols(kv_hbm[i], whole, 1 - core, g), dst, kv_snd.at[0, g, i], kv_rcv.at[0, g, i], partner)
            )
        return copies

    def kv_one(g):
        copies = []
        for which in range(2):
            for i in range(2):
                dst = kv_ref.at[i, g, pl.ds(pl.multiple_of(384 + core * 256, 128), 256), :]
                copies.append(
                    remote(
                        kv_cols(kv_hbm[i], whole, which, g), dst,
                        kv_snd.at[1 + which, g, i], kv_rcv.at[1 + core, g, i], at(p, 1, which),
                    )
                )
        return copies

    def kv_two(g, late):
        copies = []
        for which in range(2):
            for i in range(2):
                rows = pl.ds(128, 128) if late == 0 else whole
                to = pl.ds(0, 128) if late == 0 else pl.ds(128, 256)
                copies.append(
                    remote(
                        kv_cols(kv_hbm[i], rows, which, g), kv_ref.at[i, g, to, :],
                        kv_snd.at[3 + which, g, i], kv_rcv.at[3 + late, g, i], at(p, 2, which),
                    )
                )
        return copies

    for g in range(2):
        for copy in kv_one(g):
            copy.start()
        for late in range(2):
            @pl.when(core == late)
            def _():
                for copy in kv_two(g, late):
                    copy.start()
        for copy in kv_own(g) + io_copies(g):
            copy.start()

    acc_ref[...] = jnp.zeros_like(acc_ref)
    keep = jnp.where(p == 0, 0.0, 1.0).astype(F32)
    causal = lax.broadcasted_iota(jnp.int32, (BLK, 256), 0) <= lax.rem(
        lax.broadcasted_iota(jnp.int32, (BLK, 256), 1), BLK
    )

    def take_group(g):
        for i in range(2):
            pltpu.make_async_copy(io_buf[i].at[g, whole, :], io_buf[i].at[g, whole, :], io_loc.at[g, i]).wait()
            pltpu.make_async_copy(io_buf[i].at[g, whole, :], io_buf[i].at[g, whole, :], io_rcv.at[g, i]).wait()
            here = kv_ref.at[i, g, whole, :]
            half = kv_ref.at[i, g, pl.ds(0, 128), :]
            pltpu.make_async_copy(here, here, kv_loc.at[g, i]).wait()
            for source in (0, 1, 2, 4):
                pltpu.make_async_copy(here, here, kv_rcv.at[source, g, i]).wait()
            pltpu.make_async_copy(half, half, kv_rcv.at[3, g, i]).wait()
        for i in range(2):
            kvt_ref[i, g] = kv_ref[i, g].T

    def pair(g, qb, hp, hide):
        row = pl.multiple_of(qb * BLK, BLK)
        win = pl.ds(row, WIN)
        blk = pl.ds(row, BLK)
        cols = pl.ds(hp * 256, 256)
        lo, hi = slice(hp * 256, hp * 256 + 128), slice(hp * 256 + 128, hp * 256 + 256)
        q2 = jnp.concatenate([qb_ref[g, blk, lo], qb_ref[g, blk, hi]], 0)
        q2_ref[cols, :] = q2
        s_ref[hp] = dot(kv_ref[0, g, win, :], q2, ((1,), (1,)))
        top = None
        for kb in range(8):
            rows = slice(kb * BLK, (kb + 1) * BLK)
            tile = s_ref[hp, rows, :]
            if kb == 7:
                tile = jnp.where(causal, tile, -HIDE)
                s_ref[hp, rows, :] = tile
            high = jnp.max(tile, axis=0, keepdims=True)
            if kb < 7:
                high = high - hide[kb]
            top = high if top is None else jnp.maximum(top, high)
        top = top * SCALE2
        total = jnp.zeros((1, 256), F32)
        for kb in range(8):
            rows = slice(kb * BLK, (kb + 1) * BLK)
            off = top + hide[kb] if kb < 7 else top
            e = jnp.exp2(s_ref[hp, rows, :] * SCALE2 - off)
            total = total + jnp.sum(e, axis=0, keepdims=True)
            e_ref[rows, cols] = e.astype(BF16)
        inv = 1.0 / total
        ot = dot(kvt_ref[1, g, :, win], e_ref[:, cols], ((1,), (0,))) * inv
        o_st[g, blk, lo] = ot[:, :128].T.astype(BF16)
        o_st[g, blk, hi] = ot[:, 128:].T.astype(BF16)
        g2 = jnp.concatenate([gb_ref[g, blk, lo], gb_ref[g, blk, hi]], 0)
        gtn = (g2.astype(F32).T * inv).astype(BF16)
        rd = jnp.sum(ot.astype(BF16).astype(F32) * gtn.astype(F32), axis=0, keepdims=True)
        dgn_ref[cols, :] = gtn.astype(F32).T.astype(BF16)
        dp_ref[hp] = dot(kv_ref[1, g, win, :], gtn, ((1,), (0,)))
        for kb in range(8):
            rows = slice(kb * BLK, (kb + 1) * BLK)
            ds_ref[rows, cols] = (e_ref[rows, cols].astype(F32) * (dp_ref[hp, rows, :] - rd)).astype(BF16)
        qt = dot(kvt_ref[0, g, :, win], ds_ref[:, cols], ((1,), (0,))) * (SCALE * keep)
        dq_st[g, blk, lo] = qt[:, :128].T.astype(BF16)
        dq_st[g, blk, hi] = qt[:, 128:].T.astype(BF16)

    def head_cols(g):
        return pl.ds(pl.multiple_of((2 * core + g) * 512, 512), 512)

    def dq_copy(g, qb):
        half = lax.rem(qb, 2)
        return remote(
            dq_st.at[g, pl.ds(pl.multiple_of(qb * BLK, BLK), BLK), :],
            gq_ref.at[0, pl.ds(pl.multiple_of(half * BLK, BLK), BLK), head_cols(g)],
            dq_snd.at[g * 4 + qb], dq_rcv.at[core * 4 + g * 2 + half], at(prv_p, 0, lax.div(qb, 2)),
        )

    def o_copy(g, qb, local):
        half = lax.rem(qb, 2)
        src = o_st.at[g, pl.ds(pl.multiple_of(qb * BLK, BLK), BLK), :]
        dst = out_ref.at[0, pl.ds(pl.multiple_of(half * BLK, BLK), BLK), head_cols(g)]
        if local:
            return pltpu.make_async_copy(src, dst, o_sem.at[g * 4 + qb])
        return remote(src, dst, o_sem.at[g * 4 + qb], o_rcv.at[g * 2 + half], partner)

    def c2_copy(g, i):
        return remote(c2_st.at[g, i], c2_rx.at[g, i], c2_snd.at[g, i], c2_rcv.at[g, i], at(p, -2, core))

    def kv_final(g, i, which, stage, landing, snd, rcv, hop):
        return remote(
            stage.at[g, i, pl.ds(which * 256, 256), :],
            landing.at[i, :, pl.ds(pl.multiple_of((2 * core + g) * BLK, BLK), BLK)],
            snd.at[g, i, which], rcv.at[2 * core + g, i], at(prv_p, hop, which),
        )

    def c1_copy(g, i, which):
        return kv_final(g, i, which, c1_st, nxt_rx, c1_snd, c1_rcv, -1)

    def own_copy(g, i, which):
        return kv_final(g, i, which, own_st, own_rx, own_snd, own_rcv, 0)

    factor = (SCALE, 1.0)

    def send_own(g):
        for i in range(2):
            c2_copy(g, i).wait_recv()
            own_st[g, i, 0:128, :] = (acc_ref[i, g, 896:1024, :] * (factor[i] * keep)).astype(BF16)
            rest = acc_ref[i, g, 1024:1408, :] * factor[i] + c2_rx[g, i].astype(F32)
            own_st[g, i, 128:512, :] = (rest * keep).astype(BF16)
            for which in range(2):
                own_copy(g, i, which).start()

    def step(it, carry):
        g = lax.div(it, 4)
        qb = lax.rem(it, 4)

        @pl.when(qb == 0)
        def _():
            take_group(g)

        own_doc = doc_ref[0, 4 * chip + qb]
        hide = []
        for kb in range(7):
            spot = 4 * chip + qb + kb - 7
            seen = (doc_ref[0, jnp.maximum(spot, 0)] == own_doc) & (spot >= 0)
            hide.append(jnp.where(seen, 0.0, HIDE).astype(F32))
        for hp in range(2):
            pair(g, qb, hp, hide)
        win = pl.ds(pl.multiple_of(qb * BLK, BLK), WIN)
        acc_ref[1, g, win, :] += dot(e_ref[...], dgn_ref[...], ((1,), (0,)))
        acc_ref[0, g, win, :] += dot(ds_ref[...], q2_ref[...], ((1,), (0,)))
        dq_copy(g, qb).start()

        @pl.when(lax.div(qb, 2) == core)
        def _():
            o_copy(g, qb, True).start()

        @pl.when(lax.div(qb, 2) != core)
        def _():
            o_copy(g, qb, False).start()

        @pl.when(qb == 2)
        def _():
            for i in range(2):
                c2_st[g, i] = (acc_ref[i, g, 0:384, :] * factor[i]).astype(BF16)
                c2_copy(g, i).start()

        @pl.when(qb == 3)
        def _():
            for i in range(2):
                c1_st[g, i] = (acc_ref[i, g, 384:896, :] * (factor[i] * keep)).astype(BF16)
                for which in range(2):
                    c1_copy(g, i, which).start()

        @pl.when(it == 5)
        def _():
            send_own(0)

        return carry

    lax.fori_loop(0, 8, step, 0)
    send_own(1)

    for g in range(2):
        for copy in kv_one(g):
            copy.wait_send()
        for late in range(2):
            @pl.when(core == late)
            def _():
                for copy in kv_two(g, late):
                    copy.wait_send()
        kv_own(g)[1].wait_send()
        kv_own(g)[3].wait_send()
        io_copies(g)[1].wait_send()
        io_copies(g)[3].wait_send()
        for qb in range(4):
            dq_copy(g, qb).wait_send()
            @pl.when(qb // 2 == core)
            def _():
                o_copy(g, qb, True).wait()

            @pl.when(qb // 2 != core)
            def _():
                o_copy(g, qb, False).wait_send()
        for half in range(2):
            o_copy(g, half, False).wait_recv()
        for i in range(2):
            c2_copy(g, i).wait_send()
            for which in range(2):
                c1_copy(g, i, which).wait_send()
                own_copy(g, i, which).wait_send()
    for source in range(8):
        pltpu.make_async_copy(
            dq_st.at[0, pl.ds(0, BLK), :], dq_st.at[0, pl.ds(0, BLK), :], dq_rcv.at[source]
        ).wait()
    for i in range(2):
        for source in range(4):
            piece = nxt_rx.at[i, :, pl.ds(source * BLK, BLK)]
            pltpu.make_async_copy(piece, piece, c1_rcv.at[source, i]).wait()
            piece = own_rx.at[i, :, pl.ds(source * BLK, BLK)]
            pltpu.make_async_copy(piece, piece, own_rcv.at[source, i]).wait()
    gk_ref[0] = (nxt_rx[0].astype(F32) + own_rx[0].astype(F32)).astype(BF16)
    gv_ref[0] = (nxt_rx[1].astype(F32) + own_rx[1].astype(F32)).astype(BF16)


def solution(mesh):
    sections, shards = mesh.shape["pipe"], mesh.shape["ctx"]

    def body(queries, key_rows, value_rows, out_grad, doc_blocks):
        dma = pltpu.SemaphoreType.DMA
        vmem = pltpu.VMEM
        hbm = pl.BlockSpec(memory_space=pl.ANY)
        return pl.pallas_call(
            functools.partial(kernel, sections, shards),
            out_shape=(
                jax.ShapeDtypeStruct((1, 256, 2048), BF16),
                jax.ShapeDtypeStruct((1, 256, 2048), BF16),
                jax.ShapeDtypeStruct((1, 256, 512), BF16),
                jax.ShapeDtypeStruct((1, 256, 512), BF16),
            ),
            in_specs=[pl.BlockSpec(memory_space=pltpu.SMEM), hbm, hbm, hbm, hbm],
            out_specs=(
                hbm, hbm,
                pl.BlockSpec(memory_space=vmem), pl.BlockSpec(memory_space=vmem),
            ),
            scratch_shapes=[
                vmem((2, 512, 512), BF16), vmem((2, 512, 512), BF16),
                vmem((2, 2, ROWS, BLK), BF16), vmem((2, 2, BLK, ROWS), BF16),
                vmem((2, WIN, 256), F32), vmem((2, WIN, 256), F32),
                vmem((WIN, 512), BF16), vmem((WIN, 512), BF16),
                vmem((2, 2, ROWS, BLK), F32),
                vmem((512, BLK), BF16), vmem((512, BLK), BF16),
                vmem((2, 512, 512), BF16), vmem((2, 512, 512), BF16),
                vmem((2, 2, 384, BLK), BF16), vmem((2, 2, 512, BLK), BF16), vmem((2, 2, 512, BLK), BF16),
                vmem((2, 2, 384, BLK), BF16), vmem((2, 256, 512), BF16), vmem((2, 256, 512), BF16),
                dma((2, 2)), dma((2, 2)), dma((2, 2)),
                dma((2, 2)), dma((5, 2, 2)), dma((5, 2, 2)),
                dma((8,)), dma((4,)), dma((8,)), dma((8,)),
                dma((2, 2)), dma((2, 2)), dma((2, 2, 2)), dma((4, 2)), dma((2, 2, 2)), dma((4, 2)),
            ],
            compiler_params=pltpu.CompilerParams(
                collective_id=0, has_side_effects=True, vmem_limit_bytes=48 * 1024 * 1024
            ),
        )(doc_blocks, queries, key_rows, value_rows, out_grad)

    tokens = P("pipe", "ctx", None)
    return jax.shard_map(
        body,
        mesh=mesh,
        in_specs=(tokens, tokens, tokens, tokens, P("pipe", None)),
        out_specs=(tokens, tokens, tokens, tokens),
        check_vma=False,
    )
```

time: 192 us -> 81.9 us (0.43)
  the two profiles are of different devices: /device:TPU:185 before, /device:TPU:31 now
where the time goes in v1:
time: 81.9 us; the launch traced here: 81.6 us
  Pallas kernels  72.6 us (89%)
  local copies, waits for them, and re-layouts  8.34 us (10%)
    pallas_call x1, Pallas kernels, body(): pl.pallas_call(functools.partial(kernel, sections, shards), out_shape=(ja...  72.6 us
    unnamed x14, local copies, waits for them, and re-layouts  8.34 us

profile of v1, /device:TPU:31, one launch (start us, length us, event | category | flops | bytes accessed | tf_op | source)
XLA Modules:
  0.0 81.6 jit_solution(7318455332544531161)
XLA Ops:
  0.6 0.0 copy-start
  0.6 1.2 %copy-done = bf16[1,256,2048]{2,1,0:T(8,128)(2,1)S(1)} copy-done((bf16[1,256,2048]{2,1,0:T(8,128)(2,1)S(1)}, bf16[1,256,2048]{2,1,0:T(8,128)(2,1)}, u32[]{:S(2)}) %copy-start) | copy-done | bytes 1048600
  1.9 0.0 copy-start.1
  1.9 1.2 %copy-done.1 = bf16[1,256,2048]{2,1,0:T(8,128)(2,1)S(1)} copy-done((bf16[1,256,2048]{2,1,0:T(8,128)(2,1)S(1)}, bf16[1,256,2048]{2,1,0:T(8,128)(2,1)}, u32[]{:S(2)}) %copy-start.1) | copy-done | bytes 1048600
  3.1 0.0 copy-start.2
  3.1 0.9 %copy-done.2 = bf16[1,256,512]{2,1,0:T(8,128)(2,1)S(1)} copy-done((bf16[1,256,512]{2,1,0:T(8,128)(2,1)S(1)}, bf16[1,256,512]{2,1,0:T(8,128)(2,1)}, u32[]{:S(2)}) %copy-start.2) | copy-done | bytes 262168
  4.0 0.0 copy-start.3
  4.0 0.9 %copy-done.3 = bf16[1,256,512]{2,1,0:T(8,128)(2,1)S(1)} copy-done((bf16[1,256,512]{2,1,0:T(8,128)(2,1)S(1)}, bf16[1,256,512]{2,1,0:T(8,128)(2,1)}, u32[]{:S(2)}) %copy-start.3) | copy-done | bytes 262168
  5.0 0.0 copy-start.4
  5.0 0.7 copy-done.4
  5.6 72.6 %shard_map.84 = (bf16[1,256,2048]{2,1,0:T(8,128)(2,1)S(1)}, bf16[1,256,2048]{2,1,0:T(8,128)(2,1)S(1)}, bf16[1,256,512]{2,1,0:T(8,128)(2,1)S(1)}, bf16[1,256,512]{2,1,0:T(8,128)(2,1)S(1)}) custom-call(s32[1,64]{1,0:T(1,128)S(1)} %copy-done.4, bf16[1,256,2048]{2,1,0:T(8,128)(2,1)S(1)} %copy-done, bf16[1,256,512]{2,1,0:T(8,128)(2,1)S(1)} %copy-done.2, ...), custom_call_target="tpu_custom_call" | custom-call | tf_op jit(solution)/shard_map/pallas_call | solution.py:336
  78.3 1.0 %copy.13 = bf16[1,256,2048]{2,1,0:T(8,128)(2,1)} copy(bf16[1,256,2048]{2,1,0:T(8,128)(2,1)S(1)} %get-tuple-element.8) | data formatting | bytes 2097152
  79.2 1.0 %copy.14 = bf16[1,256,2048]{2,1,0:T(8,128)(2,1)} copy(bf16[1,256,2048]{2,1,0:T(8,128)(2,1)S(1)} %get-tuple-element.9) | data formatting | bytes 2097152
  80.2 0.7 copy.15
  80.9 0.7 copy.16
Async XLA Ops:
  0.6 1.2 %copy-start = (bf16[1,256,2048]{2,1,0:T(8,128)(2,1)S(1)}, bf16[1,256,2048]{2,1,0:T(8,128)(2,1)}, u32[]{:S(2)}) copy-start(bf16[1,256,2048]{2,1,0:T(8,128)(2,1)} %q_hbm.1) | copy-start | bytes 3145732
  1.9 1.2 %copy-start.1 = (bf16[1,256,2048]{2,1,0:T(8,128)(2,1)S(1)}, bf16[1,256,2048]{2,1,0:T(8,128)(2,1)}, u32[]{:S(2)}) copy-start(bf16[1,256,2048]{2,1,0:T(8,128)(2,1)} %g_hbm.1) | copy-start | bytes 3145732
  3.1 0.9 %copy-start.2 = (bf16[1,256,512]{2,1,0:T(8,128)(2,1)S(1)}, bf16[1,256,512]{2,1,0:T(8,128)(2,1)}, u32[]{:S(2)}) copy-start(bf16[1,256,512]{2,1,0:T(8,128)(2,1)} %k_hbm.1) | copy-start | bytes 786436
  4.0 0.9 %copy-start.3 = (bf16[1,256,512]{2,1,0:T(8,128)(2,1)S(1)}, bf16[1,256,512]{2,1,0:T(8,128)(2,1)}, u32[]{:S(2)}) copy-start(bf16[1,256,512]{2,1,0:T(8,128)(2,1)} %v_hbm.1) | copy-start | bytes 786436
  5.0 0.7 copy-start.4

commit v2 on v1

v2 whole, which is shorter than its diff:
```python
import functools
import math

import jax
import jax.numpy as jnp
from jax import lax
from jax.experimental import pallas as pl
from jax.experimental.pallas import tpu as pltpu
from jax.sharding import PartitionSpec as P

MESH = pl.DeviceIdType.MESH
BF16 = jnp.bfloat16
F32 = jnp.float32
BLK = 128
SCALE = 1.0 / math.sqrt(128.0)
SCALE2 = SCALE * math.log2(math.e)
HIDE = 1e30
ROWS = 11 * BLK
WIN = 8 * BLK


def dot(a, b, dims):
    return lax.dot_general(a, b, (dims, ((), ())), preferred_element_type=F32)


def kernel(
    sections, shards,
    doc_hbm, q_hbm, k_hbm, v_hbm, g_hbm,
    out_ref, gq_ref, nxt_rx, own_rx,
    doc_ref, qb_ref, gb_ref, kv_ref, kvt_ref, s_ref, dp_ref, e_ref, ds_ref, acc_ref, dgn_ref, q2_ref,
    o_st, dq_st, c2_st, c1_st, own_st, c2_rx, rel_rx,
    doc_sem, io_loc, io_snd, io_rcv, kv_loc, kv_snd, kv_rcv, o_sem, o_rcv, dq_snd, dq_rcv,
    c2_snd, c2_rcv, rel_snd, rel_rcv, c1_snd, c1_rcv, own_snd, own_rcv,
):
    p = lax.axis_index("pipe")
    dev = lax.axis_index("ctx")
    core = lax.rem(dev, 2)
    chip = lax.div(dev, 2)
    chips = shards // 2
    pair_p = p + 1 - 2 * lax.rem(p, 2)
    even = lax.rem(p, 2) == 0
    has_prev, has_prev2 = chip >= 1, chip >= 2
    has_next, has_next2 = chip <= chips - 2, chip <= chips - 3
    sends_pipe, gets_pipe = p >= 1, p <= sections - 2
    sends_relay = even & (p >= 2) & has_prev
    gets_relay = even & (p <= sections - 3) & has_prev
    sends_last = ((p <= sections - 3) | (lax.rem(p, 2) == 1)) & has_prev
    gets_last = gets_pipe & has_next

    def at(section, hop, which):
        return (section, 2 * (chip + hop) + which)

    doc_copy = pltpu.make_async_copy(doc_hbm, doc_ref, doc_sem)
    doc_copy.start()
    partner = (p, 2 * chip + 1 - core)
    barrier = pltpu.get_barrier_semaphore()

    def greet(when, targets):
        @pl.when(when)
        def _():
            for target in targets():
                pl.semaphore_signal(barrier, inc=1, device_id=target, device_id_type=MESH)

    pl.semaphore_signal(barrier, inc=1, device_id=partner, device_id_type=MESH)
    greet(has_prev, lambda: [at(p, -1, which) for which in range(2)])
    greet(has_prev2, lambda: [at(p, -2, which) for which in range(2)])
    greet(has_next2, lambda: [at(p, 2, core)])
    greet(gets_pipe, lambda: [at(p + 1, 0, which) for which in range(2)])
    greet(gets_relay, lambda: [at(p + 2, 0, core)])
    greet(gets_last, lambda: [at(pair_p, 1, which) for which in range(2)])

    @pl.when(chip < 2)
    def _():
        kv_ref[:, :, 0:384, :] = jnp.zeros((2, 2, 384, BLK), BF16)

    @pl.when(chip < 1)
    def _():
        kv_ref[:, :, 384:896, :] = jnp.zeros((2, 2, 512, BLK), BF16)

    awaited = 1
    for when, count in ((has_next, 2), (has_next2, 2), (has_prev2, 1), (sends_pipe, 2), (sends_relay, 1), (sends_last, 2)):
        awaited = awaited + jnp.where(when, count, 0)
    pl.semaphore_wait(barrier, awaited)

    def remote(src, dst, snd, rcv, target):
        return pltpu.make_async_remote_copy(
            src_ref=src, dst_ref=dst, send_sem=snd, recv_sem=rcv,
            device_id=target, device_id_type=MESH,
        )

    def kv_cols(ref, rows, which, g):
        return ref.at[0, rows, pl.ds(pl.multiple_of((2 * which + g) * BLK, BLK), BLK)]

    kv_hbm = (k_hbm, v_hbm)
    io_hbm = (q_hbm, g_hbm)
    io_buf = (qb_ref, gb_ref)
    mine = pl.ds(pl.multiple_of(core * 256, 256), 256)
    whole = pl.ds(0, 256)

    def io_copies(g):
        copies = []
        for i in range(2):
            src = lambda which: io_hbm[i].at[0, :, pl.ds(pl.multiple_of(which * 1024 + g * 512, 512), 512)]
            dst = io_buf[i].at[g, mine, :]
            copies.append(pltpu.make_async_copy(src(core), dst, io_loc.at[g, i]))
            copies.append(remote(src(1 - core), dst, io_snd.at[g, i], io_rcv.at[g, i], partner))
        return copies

    def kv_own(g):
        copies = []
        for i in range(2):
            dst = kv_ref.at[i, g, pl.ds(pl.multiple_of(896 + core * 256, 128), 256), :]
            copies.append(pltpu.make_async_copy(kv_cols(kv_hbm[i], whole, core, g), dst, kv_loc.at[g, i]))
            copies.append(
                remote(kv_cols(kv_hbm[i], whole, 1 - core, g), dst, kv_snd.at[0, g, i], kv_rcv.at[0, g, i], partner)
            )
        return copies

    def kv_one(g):
        copies = []
        for which in range(2):
            for i in range(2):
                dst = kv_ref.at[i, g, pl.ds(pl.multiple_of(384 + core * 256, 128), 256), :]
                copies.append(
                    remote(
                        kv_cols(kv_hbm[i], whole, which, g), dst,
                        kv_snd.at[1 + which, g, i], kv_rcv.at[1 + core, g, i], at(p, 1, which),
                    )
                )
        return copies

    def kv_two(g, late):
        copies = []
        for which in range(2):
            for i in range(2):
                rows = pl.ds(128, 128) if late == 0 else whole
                to = pl.ds(0, 128) if late == 0 else pl.ds(128, 256)
                copies.append(
                    remote(
                        kv_cols(kv_hbm[i], rows, which, g), kv_ref.at[i, g, to, :],
                        kv_snd.at[3 + which, g, i], kv_rcv.at[3 + late, g, i], at(p, 2, which),
                    )
                )
        return copies

    for g in range(2):
        @pl.when(has_next)
        def _():
            for copy in kv_one(g):
                copy.start()

        for copy in kv_own(g) + io_copies(g):
            copy.start()

    acc_ref[...] = jnp.zeros_like(acc_ref)

    @pl.when(jnp.logical_not(has_next2))
    def _():
        c2_rx[...] = jnp.zeros_like(c2_rx)

    causal = lax.broadcasted_iota(jnp.int32, (BLK, 256), 0) <= lax.rem(
        lax.broadcasted_iota(jnp.int32, (BLK, 256), 1), BLK
    )

    def landed(ref, sem):
        pltpu.make_async_copy(ref, ref, sem).wait()

    def take_near(g):
        for i in range(2):
            landed(io_buf[i].at[g, whole, :], io_loc.at[g, i])
            landed(io_buf[i].at[g, whole, :], io_rcv.at[g, i])
            landed(kv_ref.at[i, g, whole, :], kv_loc.at[g, i])
            landed(kv_ref.at[i, g, whole, :], kv_rcv.at[0, g, i])

            @pl.when(has_prev)
            def _():
                landed(kv_ref.at[i, g, whole, :], kv_rcv.at[1, g, i])
                landed(kv_ref.at[i, g, whole, :], kv_rcv.at[2, g, i])
        for i in range(2):
            kvt_ref[i, g, :, 384:1408] = kv_ref[i, g, 384:1408, :].T

    def take_far(g):
        @pl.when(has_prev2)
        def _():
            for i in range(2):
                landed(kv_ref.at[i, g, pl.ds(0, 128), :], kv_rcv.at[3, g, i])
                landed(kv_ref.at[i, g, whole, :], kv_rcv.at[4, g, i])
        for i in range(2):
            kvt_ref[i, g, :, 0:384] = kv_ref[i, g, 0:384, :].T

    def lanes(hp):
        return slice(hp * 256, hp * 256 + 128), slice(hp * 256 + 128, hp * 256 + 256)

    def block(g, qb, hide):
        row = pl.multiple_of(qb * BLK, BLK)
        win = pl.ds(row, WIN)
        blk = pl.ds(row, BLK)
        tiles = [slice(kb * BLK, (kb + 1) * BLK) for kb in range(8)]
        top, total, inv, ot, gtn, rd = ([None, None] for _ in range(6))

        def cols(hp):
            return pl.ds(hp * 256, 256)

        def stack(ref, hp):
            lo, hi = lanes(hp)
            return jnp.concatenate([ref[g, blk, lo], ref[g, blk, hi]], 0)

        def scores(hp, part):
            if part == 0:
                q2_ref[cols(hp), :] = stack(qb_ref, hp)
            here = pl.ds(pl.multiple_of(row + part * 512, BLK), 512)
            s_ref[hp, part * 512:part * 512 + 512, :] = dot(kv_ref[0, g, here, :], q2_ref[cols(hp), :], ((1,), (1,)))

        def highs(hp, kbs):
            for kb in kbs:
                tile = s_ref[hp, tiles[kb], :]
                if kb == 7:
                    tile = jnp.where(causal, tile, -HIDE)
                    s_ref[hp, tiles[kb], :] = tile
                high = jnp.max(tile, axis=0, keepdims=True)
                if kb < 7:
                    high = high - hide[kb]
                top[hp] = high if top[hp] is None else jnp.maximum(top[hp], high)

        def exps(hp, kbs):
            for kb in kbs:
                off = top[hp] * SCALE2
                off = off + hide[kb] if kb < 7 else off
                e = jnp.exp2(s_ref[hp, tiles[kb], :] * SCALE2 - off)
                part = jnp.sum(e, axis=0, keepdims=True)
                total[hp] = part if total[hp] is None else total[hp] + part
                e_ref[tiles[kb], cols(hp)] = e.astype(BF16)

        def attend(hp):
            lo, hi = lanes(hp)
            inv[hp] = 1.0 / total[hp]
            gtn[hp] = (stack(gb_ref, hp).astype(F32).T * inv[hp]).astype(BF16)
            dgn_ref[cols(hp), :] = gtn[hp].astype(F32).T.astype(BF16)
            ot[hp] = dot(kvt_ref[1, g, :, win], e_ref[:, cols(hp)], ((1,), (0,))) * inv[hp]
            o_st[g, blk, lo] = ot[hp][:, :128].T.astype(BF16)
            o_st[g, blk, hi] = ot[hp][:, 128:].T.astype(BF16)
            rd[hp] = jnp.sum(ot[hp].astype(BF16).astype(F32) * gtn[hp].astype(F32), axis=0, keepdims=True)

        def prob_grads(hp):
            dp_ref[hp] = dot(kv_ref[1, g, win, :], gtn[hp], ((1,), (0,)))

        def score_grads(hp, kbs):
            for kb in kbs:
                ds_ref[tiles[kb], cols(hp)] = e_ref[tiles[kb], cols(hp)] * (dp_ref[hp, tiles[kb], :] - rd[hp]).astype(BF16)

        def query_grads(hp):
            lo, hi = lanes(hp)
            qt = dot(kvt_ref[0, g, :, win], ds_ref[:, cols(hp)], ((1,), (0,))) * SCALE
            dq_st[g, blk, lo] = qt[:, :128].T.astype(BF16)
            dq_st[g, blk, hi] = qt[:, 128:].T.astype(BF16)

        early, late = range(4), range(4, 8)
        scores(0, 0)
        scores(0, 1)
        highs(0, range(8))
        scores(1, 0)
        exps(0, early)
        scores(1, 1)
        exps(0, late)
        attend(0)
        highs(1, range(8))
        prob_grads(0)
        exps(1, range(8))
        score_grads(0, range(8))
        attend(1)
        prob_grads(1)
        query_grads(0)
        score_grads(1, range(8))
        acc_ref[1, g, win, :] += dot(e_ref[...], dgn_ref[...], ((1,), (0,)))
        query_grads(1)
        acc_ref[0, g, win, :] += dot(ds_ref[...], q2_ref[...], ((1,), (0,)))

    def head_cols(g):
        return pl.ds(pl.multiple_of((2 * core + g) * 512, 512), 512)

    def dq_copy(g, qb):
        half = lax.rem(qb, 2)
        return remote(
            dq_st.at[g, pl.ds(pl.multiple_of(qb * BLK, BLK), BLK), :],
            gq_ref.at[0, pl.ds(pl.multiple_of(half * BLK, BLK), BLK), head_cols(g)],
            dq_snd.at[g * 4 + qb], dq_rcv.at[core * 4 + g * 2 + half], at(p - 1, 0, lax.div(qb, 2)),
        )

    def o_copy(g, qb, local):
        half = lax.rem(qb, 2)
        src = o_st.at[g, pl.ds(pl.multiple_of(qb * BLK, BLK), BLK), :]
        dst = out_ref.at[0, pl.ds(pl.multiple_of(half * BLK, BLK), BLK), head_cols(g)]
        if local:
            return pltpu.make_async_copy(src, dst, o_sem.at[g * 4 + qb])
        return remote(src, dst, o_sem.at[g * 4 + qb], o_rcv.at[g * 2 + half], partner)

    def c2_copy(g, i):
        return remote(c2_st.at[g, i], c2_rx.at[g, i], c2_snd.at[g, i], c2_rcv.at[g, i], at(p, -2, core))

    def rel_copy(g, i):
        return remote(c1_st.at[g, i], rel_rx.at[g, i], rel_snd.at[g, i], rel_rcv.at[g, i], at(p - 2, 0, core))

    def kv_final(g, i, which, stage, landing, snd, rcv, target):
        return remote(
            stage.at[g, i, pl.ds(which * 256, 256), :],
            landing.at[i, :, pl.ds(pl.multiple_of((2 * core + g) * BLK, BLK), BLK)],
            snd.at[g, i, which], rcv.at[2 * core + g, i], target,
        )

    def last_copy(g, i, which, stage):
        return kv_final(g, i, which, stage, nxt_rx, c1_snd, c1_rcv, at(pair_p, -1, which))

    def own_copy(g, i, which):
        return kv_final(g, i, which, own_st, own_rx, own_snd, own_rcv, at(p - 1, 0, which))

    factor = (SCALE, 1.0)

    def send_own(g):
        @pl.when(has_next2)
        def _():
            for i in range(2):
                c2_copy(g, i).wait_recv()

        @pl.when(sends_pipe)
        def _():
            for i in range(2):
                own_st[g, i, 0:128, :] = (acc_ref[i, g, 896:1024, :] * factor[i]).astype(BF16)
                rest = acc_ref[i, g, 1024:1408, :] * factor[i] + c2_rx[g, i].astype(F32)
                own_st[g, i, 128:512, :] = rest.astype(BF16)
                for which in range(2):
                    own_copy(g, i, which).start()

    def forward(g):
        @pl.when(gets_relay)
        def _():
            for i in range(2):
                rel_copy(g, i).wait_recv()
                for which in range(2):
                    last_copy(g, i, which, rel_rx).start()

    def step(it, carry):
        g = jnp.where((it == 1) | (it >= 5), 1, 0)
        qb = jnp.where(it < 2, 3, jnp.where(it < 5, 4 - it, 7 - it))

        @pl.when(it < 2)
        def _():
            take_near(g)

        @pl.when(it == 0)
        def _():
            for late in range(2):
                @pl.when(has_next2 & (core == late))
                def _():
                    for group in range(2):
                        for copy in kv_two(group, late):
                            copy.start()

        @pl.when((it == 2) | (it == 5))
        def _():
            take_far(g)

        own_doc = doc_ref[0, 4 * chip + qb]
        hide = []
        for kb in range(7):
            spot = 4 * chip + qb + kb - 7
            seen = (doc_ref[0, jnp.maximum(spot, 0)] == own_doc) & (spot >= 0)
            hide.append(jnp.where(seen, 0.0, HIDE).astype(F32))
        block(g, qb, hide)

        @pl.when(sends_pipe)
        def _():
            dq_copy(g, qb).start()

        @pl.when(lax.div(qb, 2) == core)
        def _():
            o_copy(g, qb, True).start()

        @pl.when(lax.div(qb, 2) != core)
        def _():
            o_copy(g, qb, False).start()

        done = (it == 4) | (it == 7)

        @pl.when(done & has_prev2)
        def _():
            for i in range(2):
                c2_st[g, i] = (acc_ref[i, g, 0:384, :] * factor[i]).astype(BF16)
                c2_copy(g, i).start()

        @pl.when(done & has_prev & sends_pipe)
        def _():
            for i in range(2):
                c1_st[g, i] = (acc_ref[i, g, 384:896, :] * factor[i]).astype(BF16)

                @pl.when(even)
                def _():
                    rel_copy(g, i).start()

                @pl.when(jnp.logical_not(even))
                def _():
                    for which in range(2):
                        last_copy(g, i, which, c1_st).start()

        @pl.when(it == 6)
        def _():
            send_own(0)
            forward(0)

        return carry

    doc_copy.wait()
    lax.fori_loop(0, 8, step, 0)
    send_own(1)
    forward(1)

    for g in range(2):
        @pl.when(has_next)
        def _():
            for copy in kv_one(g):
                copy.wait_send()

        for late in range(2):
            @pl.when(has_next2 & (core == late))
            def _():
                for copy in kv_two(g, late):
                    copy.wait_send()
        for copy in kv_own(g)[1::2] + io_copies(g)[1::2]:
            copy.wait_send()
        for qb in range(4):
            @pl.when(qb // 2 == core)
            def _():
                o_copy(g, qb, True).wait()

            @pl.when(qb // 2 != core)
            def _():
                o_copy(g, qb, False).wait_send()
        for half in range(2):
            o_copy(g, half, False).wait_recv()

        @pl.when(has_prev2)
        def _():
            for i in range(2):
                c2_copy(g, i).wait_send()

        @pl.when(sends_relay)
        def _():
            for i in range(2):
                rel_copy(g, i).wait_send()

        @pl.when(sends_last)
        def _():
            for i in range(2):
                for which in range(2):
                    last_copy(g, i, which, rel_rx).wait_send()

        @pl.when(sends_pipe)
        def _():
            for qb in range(4):
                dq_copy(g, qb).wait_send()
            for i in range(2):
                for which in range(2):
                    own_copy(g, i, which).wait_send()

    @pl.when(gets_pipe)
    def _():
        for source in range(8):
            landed(dq_st.at[0, pl.ds(0, BLK), :], dq_rcv.at[source])
        for i in range(2):
            for source in range(4):
                landed(own_rx.at[i, :, pl.ds(source * BLK, BLK)], own_rcv.at[source, i])

    @pl.when(gets_last)
    def _():
        for i in range(2):
            for source in range(4):
                landed(nxt_rx.at[i, :, pl.ds(source * BLK, BLK)], c1_rcv.at[source, i])


def finish(sections, shards, out_ref, gq_ref, nxt_ref, own_ref, out_hbm, gq_hbm, gk_hbm, gv_hbm, sum_ref, zero_ref, sems):
    gets_pipe = lax.axis_index("pipe") <= sections - 2
    gets_last = gets_pipe & (lax.axis_index("ctx") < shards - 2)
    out_copy = pltpu.make_async_copy(out_ref, out_hbm, sems.at[0])
    out_copy.start()

    @pl.when(gets_pipe)
    def _():
        pltpu.make_async_copy(gq_ref, gq_hbm, sems.at[1]).start()

    @pl.when(jnp.logical_not(gets_pipe))
    def _():
        zero_ref[...] = jnp.zeros_like(zero_ref)
        pltpu.make_async_copy(zero_ref, gq_hbm, sems.at[1]).start()

    grads = (gk_hbm, gv_hbm)
    for i in range(2):
        last = jnp.where(gets_last, nxt_ref[i].astype(F32), 0.0)
        sum_ref[i] = jnp.where(gets_pipe, last + own_ref[i].astype(F32), 0.0).astype(BF16)
        pltpu.make_async_copy(sum_ref.at[pl.ds(i, 1)], grads[i], sems.at[2 + i]).start()
    out_copy.wait()
    pltpu.make_async_copy(zero_ref, gq_hbm, sems.at[1]).wait()
    for i in range(2):
        pltpu.make_async_copy(sum_ref.at[pl.ds(i, 1)], grads[i], sems.at[2 + i]).wait()


def solution(mesh):
    sections, shards = mesh.shape["pipe"], mesh.shape["ctx"]

    def body(queries, key_rows, value_rows, out_grad, doc_blocks):
        dma = pltpu.SemaphoreType.DMA
        vmem = pltpu.VMEM
        hbm = pl.BlockSpec(memory_space=pltpu.HBM)
        near = pl.BlockSpec(memory_space=vmem)
        any_place = pl.BlockSpec(memory_space=pl.ANY)
        wide = jax.ShapeDtypeStruct((1, 256, 2048), BF16)
        slim = jax.ShapeDtypeStruct((1, 256, 512), BF16)
        both = jax.ShapeDtypeStruct((2, 256, 512), BF16)
        pinned = [pltpu.with_memory_space_constraint(x, pltpu.HBM) for x in (doc_blocks, queries, key_rows, value_rows, out_grad)]
        parts = pl.pallas_call(
            functools.partial(kernel, sections, shards),
            out_shape=(wide, wide, both, both),
            in_specs=[hbm] * 5,
            out_specs=(any_place,) * 4,
            scratch_shapes=[
                pltpu.SMEM((1, 64), jnp.int32),
                vmem((2, 512, 512), BF16), vmem((2, 512, 512), BF16),
                vmem((2, 2, ROWS, BLK), BF16), vmem((2, 2, BLK, ROWS), BF16),
                vmem((2, WIN, 256), F32), vmem((2, WIN, 256), F32),
                vmem((WIN, 512), BF16), vmem((WIN, 512), BF16),
                vmem((2, 2, ROWS, BLK), F32),
                vmem((512, BLK), BF16), vmem((512, BLK), BF16),
                vmem((2, 512, 512), BF16), vmem((2, 512, 512), BF16),
                vmem((2, 2, 384, BLK), BF16), vmem((2, 2, 512, BLK), BF16), vmem((2, 2, 512, BLK), BF16),
                vmem((2, 2, 384, BLK), BF16), vmem((2, 2, 512, BLK), BF16),
                dma, dma((2, 2)), dma((2, 2)), dma((2, 2)),
                dma((2, 2)), dma((5, 2, 2)), dma((5, 2, 2)),
                dma((8,)), dma((4,)), dma((8,)), dma((8,)),
                dma((2, 2)), dma((2, 2)), dma((2, 2)), dma((2, 2)),
                dma((2, 2, 2)), dma((4, 2)), dma((2, 2, 2)), dma((4, 2)),
            ],
            compiler_params=pltpu.CompilerParams(
                collective_id=0, has_side_effects=True, vmem_limit_bytes=48 * 1048576
            ),
        )(*pinned)
        return pl.pallas_call(
            functools.partial(finish, sections, shards),
            out_shape=(wide, wide, slim, slim),
            in_specs=[any_place, any_place, near, near],
            out_specs=(hbm,) * 4,
            scratch_shapes=[vmem((2, 256, 512), BF16), vmem((1, 256, 2048), BF16), dma((4,))],
            compiler_params=pltpu.CompilerParams(vmem_limit_bytes=8 * 1048576),
        )(*parts)

    tokens = P("pipe", "ctx", None)
    return jax.shard_map(
        body,
        mesh=mesh,
        in_specs=(tokens, tokens, tokens, tokens, P("pipe", None)),
        out_specs=(tokens, tokens, tokens, tokens),
        check_vma=False,
    )
```

time: 81.9 us -> 56.7 us (0.69)
  the two profiles are of different devices: /device:TPU:31 before, /device:TPU:55 now
where the time goes in v2:
time: 56.7 us; the launch traced here: 56.6 us
  Pallas kernels  56 us (99%)
  between operations  0.64 us (1%)
    pallas_call x1, Pallas kernels, body(): pl.pallas_call(functools.partial(kernel, sections, shards), out_shape=(wi...  54.4 us
    pallas_call x1, Pallas kernels, body(): pl.pallas_call(functools.partial(finish, sections, shards), out_shape=(wi...  1.52 us

profile of v2, /device:TPU:55, one launch (start us, length us, event | category | flops | bytes accessed | tf_op | source)
XLA Modules:
  0.0 56.6 jit_solution(10341896809030813919)
XLA Ops:
  0.6 54.4 %shard_map.84 = (bf16[1,256,2048]{2,1,0:T(8,128)(2,1)S(1)}, bf16[1,256,2048]{2,1,0:T(8,128)(2,1)S(1)}, bf16[2,256,512]{2,1,0:T(8,128)(2,1)S(1)}, bf16[2,256,512]{2,1,0:T(8,128)(2,1)S(1)}) custom-call(s32[1,64]{1,0:T(1,128)} %doc_hbm.1, bf16[1,256,2048]{2,1,0:T(8,128)(2,1)} %q_hbm.1, bf16[1,256,512]{2,1,0:T(8,128)(2,1)} %k_hbm.1, bf16[1,256,512]{2,1,0:T(8,128)(2,1)} %v_hbm.1, ...), custom_call_target="tpu_custom_call" | custom-call | tf_op jit(solution)/shard_map/pallas_call | solution.py:518
  55.1 1.5 %shard_map.85 = (bf16[1,256,2048]{2,1,0:T(8,128)(2,1)}, bf16[1,256,2048]{2,1,0:T(8,128)(2,1)}, bf16[1,256,512]{2,1,0:T(8,128)(2,1)}, bf16[1,256,512]{2,1,0:T(8,128)(2,1)}) custom-call(bf16[1,256,2048]{2,1,0:T(8,128)(2,1)S(1)} %get-tuple-element.8.out_ref, bf16[1,256,2048]{2,1,0:T(8,128)(2,1)S(1)} %get-tuple-element.9.gq_ref, ...), custom_call_target="tpu_custom_call" | custom-call | tf_op jit(solution)/shard_map/pallas_call | solution.py:544

commit v3 on v2

--- a/solution.py
+++ b/solution.py
@@ -271,8 +271,13 @@
         prob_grads(1)
         query_grads(0)
         score_grads(1, range(8))
+        query_grads(1)
+
+        @pl.when(sends_pipe)
+        def _():
+            dq_copy(g, qb).start()
+
         acc_ref[1, g, win, :] += dot(e_ref[...], dgn_ref[...], ((1,), (0,)))
-        query_grads(1)
         acc_ref[0, g, win, :] += dot(ds_ref[...], q2_ref[...], ((1,), (0,)))
 
     def head_cols(g):
@@ -366,10 +371,6 @@
             seen = (doc_ref[0, jnp.maximum(spot, 0)] == own_doc) & (spot >= 0)
             hide.append(jnp.where(seen, 0.0, HIDE).astype(F32))
         block(g, qb, hide)
-
-        @pl.when(sends_pipe)
-        def _():
-            dq_copy(g, qb).start()
 
         @pl.when(lax.div(qb, 2) == core)
         def _():

time: 56.7 us -> 58.4 us (1.030)
  Pallas kernels: 56 us -> 57.7 us
    pallas_call x1, Pallas kernels: 54.4 us -> 56.2 us  [body(): pl.pallas_call(functools.partial(kernel, sections, shards), out_shape=(wi...]
where the time goes in v3:
time: 58.4 us; the launch traced here: 58.3 us
  Pallas kernels  57.7 us (99%)
  between operations  0.64 us (1%)
    pallas_call x1, Pallas kernels, body(): pl.pallas_call(functools.partial(kernel, sections, shards), out_shape=(wi...  56.2 us
    pallas_call x1, Pallas kernels, body(): pl.pallas_call(functools.partial(finish, sections, shards), out_shape=(wi...  1.52 us

profile of v3, /device:TPU:55, one launch (start us, length us, event | category | flops | bytes accessed | tf_op | source)
XLA Modules:
  0.0 58.3 jit_solution(1119596292424870435)
XLA Ops:
  0.6 56.2 %shard_map.84 = (bf16[1,256,2048]{2,1,0:T(8,128)(2,1)S(1)}, bf16[1,256,2048]{2,1,0:T(8,128)(2,1)S(1)}, bf16[2,256,512]{2,1,0:T(8,128)(2,1)S(1)}, bf16[2,256,512]{2,1,0:T(8,128)(2,1)S(1)}) custom-call(s32[1,64]{1,0:T(1,128)} %doc_hbm.1, bf16[1,256,2048]{2,1,0:T(8,128)(2,1)} %q_hbm.1, bf16[1,256,512]{2,1,0:T(8,128)(2,1)} %k_hbm.1, bf16[1,256,512]{2,1,0:T(8,128)(2,1)} %v_hbm.1, ...), custom_call_target="tpu_custom_call" | custom-call | tf_op jit(solution)/shard_map/pallas_call | solution.py:519
  56.8 1.5 %shard_map.85 = (bf16[1,256,2048]{2,1,0:T(8,128)(2,1)}, bf16[1,256,2048]{2,1,0:T(8,128)(2,1)}, bf16[1,256,512]{2,1,0:T(8,128)(2,1)}, bf16[1,256,512]{2,1,0:T(8,128)(2,1)}) custom-call(bf16[1,256,2048]{2,1,0:T(8,128)(2,1)S(1)} %get-tuple-element.8.out_ref, bf16[1,256,2048]{2,1,0:T(8,128)(2,1)S(1)} %get-tuple-element.9.gq_ref, ...), custom_call_target="tpu_custom_call" | custom-call | tf_op jit(solution)/shard_map/pallas_call | solution.py:545
